TPU v7x, 32 devices: a whole 2x2x4 slice. The times are simulated.
32 devices in a mesh: wave: 4 (over z), tile: 8 (over y, x, core).
Axes of the slice: x: 2, y: 2, z: 4, core: 2. Of those that a mesh axis runs over, the one named last changes fastest.
Arguments:
- spectral: bfloat16 [640, 2, 64, 1281], P('wave', None, 'tile'), may hold values from -0.083496094 to 0.083496094
- legendre: bfloat16 [640, 8, 1281], P('wave'), may hold values from -0.25 to 0.25
- pair_ids: int32 [640], replicated, may hold values from 0 to 639, each once
Outputs:
- spectral_out: bfloat16 [640, 2, 64, 1281], P('wave', None, 'tile')
Inputs may be any that keep to these rules, and one draw needn't show every extreme that they name: A permutation: each pair 0 to 639 appears once; slot s of spectral, legendre and spectral_out holds wavenumbers pair_ids[s] and 1279 - pair_ids[s].
All inputs are finite; a program needn't handle non-finite values.
Results may differ from a plain program's by a relative error of at most 0.0072.
Values may be sent and summed in bfloat16 or wider, within the bound.
A program may use at most 64 MiB of HBM per device.

v0:
```python
import functools
import math

import jax
import jax.numpy as jnp
from jax import lax
from jax.experimental import pallas as pl
from jax.experimental.pallas import tpu as pltpu
from jax.sharding import PartitionSpec as P

MW = 1280
HALF_LATS = 1280
PAIRS = 640
NPTS = 5156
LANES = 128
RADIX = 32

F32 = jnp.float32
BF16 = jnp.bfloat16

HALF = MW // 2
GROUP = HALF // 2
GPAD = -(-GROUP // LANES) * LANES
BLOCKS = GPAD // RADIX
SPAN = 16
AHEAD = 3
MESH = pl.DeviceIdType.MESH
NT = (((1,), (1,)), ((), ()))


def dot(a, b):
    return jnp.dot(a, b, preferred_element_type=F32)


def dot_nt(a, b):
    return lax.dot_general(a, b, NT, preferred_element_type=F32)


def middle_kernel(waves, tiles, cols, lat_count, kpad, *refs):
    (coef, ids, out, fx, gsend, grecv, psend, precv, bsend, trig_t, small_c, small_s, hot,
     s1, r1, s2, r2, s3, r3, s4, r4) = refs
    wave, tile = lax.axis_index("wave"), lax.axis_index("tile")
    quarter = NPTS // 4
    halves = 4 * kpad // tiles
    per_d = tiles // 4
    rows = 2 * cols
    slots = coef.shape[2]

    def exchange(axis, here, count, src, dst, send, recv):
        copies = []
        for off in range(1, count):
            peer = lax.rem(here + off, count)
            copy = pltpu.make_async_remote_copy(
                src_ref=src.at[peer], dst_ref=dst.at[here], send_sem=send.at[off],
                recv_sem=recv.at[off], device_id={axis: peer}, device_id_type=MESH,
            )
            copy.start()
            copies.append(copy)
        dst[here] = src[here]
        return copies

    def finish(axis, here, count, src, dst, send, recv):
        for off in range(1, count):
            origin = lax.rem(here + count - off, count)
            pltpu.make_async_remote_copy(
                src_ref=src.at[origin], dst_ref=dst.at[origin], send_sem=send.at[off],
                recv_sem=recv.at[off], device_id={axis: origin}, device_id_type=MESH,
            ).wait_recv()

    barrier = pltpu.get_barrier_semaphore()
    for axis, here, count in (("wave", wave, waves), ("tile", tile, tiles)):
        for off in range(1, count):
            pl.semaphore_signal(
                barrier, inc=1, device_id={axis: lax.rem(here + off, count)}, device_id_type=MESH
            )

    polar = wave * HALF // (lat_count // 2)
    q0 = 5 + polar
    n0, n1 = 4 * q0, NPTS - 4 * q0

    def line(shape, axis):
        return lax.broadcasted_iota(jnp.int32, shape, axis)

    k = line((1, kpad), 1)
    second = k >= q0
    inside = k < quarter
    point = jnp.where(inside, k - jnp.where(second, q0, 0), 0).astype(F32)
    length = jnp.where(second, n1, n0).astype(F32)

    def trig(m):
        whole = m.astype(F32) * point
        phase = whole - jnp.floor(whole / length) * length
        angle = (2.0 * math.pi) * phase / length
        return jnp.cos(angle), jnp.sin(angle)

    r = line((RADIX, 1), 0)
    m = jnp.where(r < 8, 2 * r, 16 * (r - 8))
    m = jnp.where(r >= 12, (r - 12) // 2 * HALF + (r - 12) % 2, m)
    m = jnp.where(r >= 16, 2 * RADIX * (r - 16), m)
    c, s = trig(m)
    outer = 4 * SPAN
    for g in range(4):
        ca, sa, cb, sb = c[16:], s[16:], c[12 + g : 13 + g], s[12 + g : 13 + g]
        small_c[g * SPAN : (g + 1) * SPAN] = ca * cb - sa * sb
        small_s[g * SPAN : (g + 1) * SPAN] = sa * cb + ca * sb
        ca, sa, cb, sb = c[:8], s[:8], c[8 + g : 9 + g], s[8 + g : 9 + g]
        small_c[outer + 8 * g : outer + 8 * g + 8] = ca * cb - sa * sb
        small_s[outer + 8 * g : outer + 8 * g + 8] = sa * cb + ca * sb

    pl.semaphore_wait(barrier, waves + tiles - 2)
    sends = exchange("wave", wave, waves, coef, fx, s1, r1)

    def block(idx, carry):
        g, a = idx // BLOCKS, idx % BLOCKS
        row_a = g * SPAN + a
        ac, as_ = small_c[pl.ds(row_a, 1), :], small_s[pl.ds(row_a, 1), :]
        bc, bs = small_c[outer:, :], small_s[outer:, :]
        at = ((g % 2) * 4 + g // 2) * GPAD + a * RADIX
        cos_at = pl.ds(pl.multiple_of(at, RADIX), RADIX)
        sin_at = pl.ds(pl.multiple_of(at + 2 * GPAD, RADIX), RADIX)
        trig_t[cos_at, :] = (ac * bc - as_ * bs).astype(BF16)
        trig_t[sin_at, :] = (as_ * bc + ac * bs).astype(BF16)
        return carry

    lax.fori_loop(0, 4 * BLOCKS, block, 0)

    lane = line((2 * GPAD, 1), 0)
    par = jnp.where(lane >= GPAD, 1, 0)
    i = lane - par * GPAD
    low = jnp.where(i < GROUP, 2 * i + par, -1)
    high = jnp.where(i < GROUP, HALF - 1 - par - 2 * i, -1)
    pair = ids[...].reshape(1, ids.shape[0])
    hot[0] = jnp.where(pair == low, 1.0, 0.0).astype(BF16)
    hot[1] = jnp.where(pair == high, 1.0, 0.0).astype(BF16)

    row = line((rows, 1), 0)
    n_row = jnp.where(row >= cols, n1, n0)
    cycle = jnp.where(row >= cols, HALF_LATS - 1 - polar, polar)
    weight = 40.0 * jnp.sin(math.pi * (cycle.astype(F32) + 0.5) / (2.0 * HALF_LATS))
    weight = weight / jnp.sqrt(lat_count * n_row.astype(F32))
    ii = line((1, GPAD), 1)
    up = ii % 2 == 0
    sign = jnp.where(up, 1.0, -1.0)

    def wavenumber(h, p):
        return h * HALF + p + 2 * ii

    def table(p):
        return trig_t[p * 4 * GPAD : (p + 1) * 4 * GPAD, :]

    finish("wave", wave, waves, coef, fx, s1, r1)
    terms = [[[], []], [[], []]]
    for h in range(2):
        here = [fx[w, h * 2 * rows : (h + 1) * 2 * rows, :] for w in range(waves)]
        both = dot_nt(jnp.concatenate(here, axis=1), hot[h])
        for p in range(2):
            m = wavenumber(h, p)
            factor = jnp.where(2 * m < n_row, jnp.where(m == 0, 1.0, 2.0), 0.0)
            part = both[:, p * GPAD : (p + 1) * GPAD]
            re, im = part[:rows] * factor, part[rows:] * factor
            cos_side, sin_side = ((re, re), (-im, -im)) if p == 0 else ((re, im), (-im, re))
            for x, (a, b) in enumerate((cos_side, sin_side)):
                terms[p][x].append(jnp.concatenate([a, b * sign]).astype(BF16))
    even = dot(jnp.concatenate(terms[0][0] + terms[0][1], axis=1), table(0))
    odd = dot(jnp.concatenate(terms[1][0] + terms[1][1], axis=1), table(1))

    def lat_of(x, v):
        return jnp.where(
            second, x[v * rows + cols : (v + 1) * rows], x[v * rows : v * rows + cols]
        )

    e0, e1, o0, o1 = lat_of(even, 0), lat_of(even, 1), lat_of(odd, 0), lat_of(odd, 1)
    for d, x in enumerate((e0 + o0, e1 - o1, e0 - o0, e1 + o1)):
        x = x.astype(BF16)
        for t in range(per_d):
            gsend[d * per_d + t] = x[:, t * halves : (t + 1) * halves]
    sends += exchange("tile", tile, tiles, gsend, grecv, s2, r2)
    finish("tile", tile, tiles, gsend, grecv, s2, r2)

    layers = cols * tiles // 4
    per_f = tiles // 4

    def field(f):
        return jnp.concatenate([grecv[f * per_f + t] for t in range(per_f)])

    u, w_, q = field(0).astype(F32), field(1).astype(F32), field(3).astype(F32)
    t16 = field(2)
    tri = jnp.where(line((layers, layers), 1) >= line((layers, layers), 0), 1.0, 0.0)
    geo = dot(tri.astype(BF16), t16) / math.sqrt(layers)
    temp = t16.astype(F32)
    for f, x in enumerate((0.5 * (u * u + w_ * w_) + geo, u * temp, w_ * temp, u * q)):
        x = x.astype(BF16)
        for t in range(per_f):
            psend[f * per_f + t] = x[t * cols : (t + 1) * cols]
    sends += exchange("tile", tile, tiles, psend, precv, s3, r3)
    finish("tile", tile, tiles, psend, precv, s3, r3)

    def quadrant(d):
        x = jnp.concatenate([precv[d * per_d + t].astype(F32) for t in range(per_d)], axis=1)
        return jnp.where(inside, x, 0.0)

    x0, x1, x2, x3 = [quadrant(d) for d in range(4)]

    def by_lat(*variants):
        return jnp.concatenate(
            [jnp.where(keep, v, 0.0) for v in variants for keep in (k < q0, second)]
        ).astype(BF16)

    even_in = by_lat((x0 + x2) + (x1 + x3), (x0 + x2) - (x1 + x3))
    odd_in = by_lat(x0 - x2, x1 - x3)
    even_out, odd_out = dot_nt(even_in, table(0)), dot_nt(odd_in, table(1))
    for h in range(2):
        at_c, at_s = slice(h * GPAD, (h + 1) * GPAD), slice((2 + h) * GPAD, (3 + h) * GPAD)
        ec, es, oc, os_ = even_out[:, at_c], even_out[:, at_s], odd_out[:, at_c], odd_out[:, at_s]
        keep_e = jnp.where(2 * wavenumber(h, 0) < n_row, weight, 0.0)
        keep_o = jnp.where(2 * wavenumber(h, 1) < n_row, weight, 0.0)
        e_re = jnp.where(up, ec[:rows], ec[rows:]) * keep_e
        e_im = -jnp.where(up, es[:rows], es[rows:]) * keep_e
        o_re = (oc[:rows] - sign * os_[rows:]) * keep_o
        o_im = (-os_[:rows] - sign * oc[rows:]) * keep_o
        e_both = jnp.concatenate([e_re, e_im]).astype(BF16)
        o_both = jnp.concatenate([o_re, o_im]).astype(BF16)
        res = (dot(e_both, hot[h, :GPAD]) + dot(o_both, hot[h, GPAD:])).astype(BF16)
        for w in range(waves):
            bsend[w, h * 2 * rows : (h + 1) * 2 * rows, :] = res[:, w * slots : (w + 1) * slots]
    sends += exchange("wave", wave, waves, bsend, out, s4, r4)
    finish("wave", wave, waves, bsend, out, s4, r4)
    for copy in sends:
        copy.wait_send()


def middle(coef, ids, waves, tiles, cols, lat_count):
    slots = coef.shape[2]
    step = max(tiles // 4, 1) * LANES
    kpad = -(-(NPTS // 4) // step) * step
    chunk = (tiles, cols, 4 * kpad // tiles)
    dma = pltpu.SemaphoreType.DMA
    vmem = pl.BlockSpec(memory_space=pltpu.VMEM)
    return pl.pallas_call(
        functools.partial(middle_kernel, waves, tiles, cols, lat_count, kpad),
        out_shape=jax.ShapeDtypeStruct(coef.shape, BF16),
        in_specs=[vmem, vmem],
        out_specs=vmem,
        scratch_shapes=[
            pltpu.VMEM(coef.shape, BF16),
            pltpu.VMEM(chunk, BF16), pltpu.VMEM(chunk, BF16),
            pltpu.VMEM(chunk, BF16), pltpu.VMEM(chunk, BF16),
            pltpu.VMEM(coef.shape, BF16),
            pltpu.VMEM((8 * GPAD, kpad), BF16),
            pltpu.VMEM((4 * SPAN + RADIX, kpad), F32),
            pltpu.VMEM((4 * SPAN + RADIX, kpad), F32),
            pltpu.VMEM((2, 2 * GPAD, waves * slots), BF16),
            dma((waves,)), dma((waves,)), dma((tiles,)), dma((tiles,)),
            dma((tiles,)), dma((tiles,)), dma((waves,)), dma((waves,)),
        ],
        compiler_params=pltpu.CompilerParams(
            collective_id=0, has_side_effects=True, vmem_limit_bytes=40 * 2**20
        ),
        name="middle",
    )(coef, ids)


def halves_of(ids, block, base):
    lane = lax.broadcasted_iota(jnp.int32, block.shape[1:], 1)
    parts = []
    for b in range(block.shape[0]):
        rows = block[b].astype(F32)
        low = lane < MW - ids[base + b]
        both = [jnp.where(low, rows, 0.0), jnp.where(low, 0.0, rows)]
        parts.append(jnp.concatenate(both).astype(BF16))
    return jnp.concatenate(parts)


def same_slot(shape, rows, columns):
    row = lax.broadcasted_iota(jnp.int32, shape, 0) // rows
    return row == lax.broadcasted_iota(jnp.int32, shape, 1) // columns


def fold(rows, columns):
    row = lax.broadcasted_iota(jnp.int32, (rows, columns), 0) % columns
    same = row == lax.broadcasted_iota(jnp.int32, (rows, columns), 1)
    return jnp.where(same, 1.0, 0.0).astype(BF16)


def forward_kernel(take, ids, spectral, legendre, out, spec_v, leg_v, spec_sem, leg_sem):
    slots, lats, row_total = legendre.shape
    fields = spectral.shape[1] * spectral.shape[2]
    base = lax.axis_index("wave") * slots
    copies = []
    for g in range(slots // take):
        at = pl.ds(g * take, take)
        pair = [
            pltpu.make_async_copy(legendre.at[at], leg_v.at[at], leg_sem.at[g]),
            pltpu.make_async_copy(spectral.at[at], spec_v.at[at], spec_sem.at[g]),
        ]
        copies.append(pair)
    for pair in copies[:AHEAD]:
        for copy in pair:
            copy.start()
    shape = (take * 2 * lats, take * fields)
    same = same_slot(shape, 2 * lats, fields)
    folded = fold(take * fields, fields)
    for g, pair in enumerate(copies):
        for copy in pair:
            copy.wait()
        for copy in copies[g + AHEAD] if g + AHEAD < len(copies) else ():
            copy.start()
        here = slice(g * take, (g + 1) * take)
        left = halves_of(ids, leg_v[here], base + g * take)
        right = spec_v[here].astype(F32).reshape(take * fields, row_total).astype(BF16)
        full = jnp.where(same, dot_nt(left, right), 0.0).astype(BF16)
        full = dot(full, folded).astype(BF16)
        out[here] = full.reshape((take,) + out.shape[1:])


def inverse_kernel(take, ids, back, legendre, out, leg_v, out_v, leg_sem, out_sem):
    slots, lats, row_total = legendre.shape
    fields = out.shape[1] * out.shape[2]
    base = lax.axis_index("wave") * slots
    copies = []
    for g in range(slots // take):
        at = pl.ds(g * take, take)
        copies.append(pltpu.make_async_copy(legendre.at[at], leg_v.at[at], leg_sem.at[g]))
        copies[-1].start()
    shape = (take * fields, take * 2 * lats)
    same = same_slot(shape, fields, 2 * lats)
    folded = fold(take * 2 * lats, 2 * lats)
    results = []
    for g, copy in enumerate(copies):
        at = pl.ds(g * take, take)
        here = slice(g * take, (g + 1) * take)
        narrow = back[here].reshape(take * fields, 2 * lats)
        wide = jnp.where(same, dot_nt(narrow, folded), 0.0).astype(BF16)
        copy.wait()
        right = halves_of(ids, leg_v[here], base + g * take)
        out_v[here] = dot(wide, right).reshape((take,) + out.shape[1:]).astype(BF16)
        results.append(pltpu.make_async_copy(out_v.at[at], out.at[at], out_sem.at[g]))
        results[-1].start()
    for copy in results:
        copy.wait()


def local(spectral, legendre, pair_ids):
    slots, _, cols, row_total = spectral.shape
    lat_count = legendre.shape[1]
    waves, tiles = lax.axis_size("wave"), lax.axis_size("tile")
    take = max(b for b in range(1, 17) if slots % b == 0)
    groups = slots // take
    smem = pl.BlockSpec(memory_space=pltpu.SMEM)
    vmem = pl.BlockSpec(memory_space=pltpu.VMEM)
    hbm = pl.BlockSpec(memory_space=pl.ANY)
    dma = pltpu.SemaphoreType.DMA((groups,))
    params = pltpu.CompilerParams(vmem_limit_bytes=60 * 2**20)
    coef = pl.pallas_call(
        functools.partial(forward_kernel, take),
        out_shape=jax.ShapeDtypeStruct((slots, 2 * lat_count, 2 * cols), BF16),
        in_specs=[smem, hbm, hbm],
        out_specs=vmem,
        scratch_shapes=[
            pltpu.VMEM(spectral.shape, BF16), pltpu.VMEM(legendre.shape, BF16), dma, dma,
        ],
        compiler_params=params,
        name="forward",
    )(pair_ids, spectral, legendre)
    coef = coef.reshape(slots, 2, waves, 2, 2, cols).transpose(2, 1, 4, 3, 5, 0)
    coef = coef.reshape(waves, 8 * cols, slots)
    back = middle(coef, pair_ids, waves, tiles, cols, lat_count)
    back = back.reshape(waves, 2, 2, 2, cols, slots).transpose(5, 2, 4, 1, 0, 3)
    back = back.reshape(slots, 2 * cols, 2 * lat_count)
    return pl.pallas_call(
        functools.partial(inverse_kernel, take),
        out_shape=jax.ShapeDtypeStruct(spectral.shape, BF16),
        in_specs=[smem, vmem, hbm],
        out_specs=hbm,
        scratch_shapes=[
            pltpu.VMEM(legendre.shape, BF16), pltpu.VMEM(spectral.shape, BF16), dma, dma,
        ],
        compiler_params=params,
        name="inverse",
    )(pair_ids, back, legendre)


def solution(mesh):
    placed = (P("wave", None, "tile", None), P("wave", None, None), P())
    return jax.shard_map(
        local, mesh=mesh, in_specs=placed, out_specs=P("wave", None, "tile", None), check_vma=False
    )
```

profile of v0, /device:TPU:0, one launch (start us, length us, event | category | flops | bytes accessed | tf_op | source)
XLA Modules:
  0.0 47.9 jit_solution(8788842695093645115)
XLA Ops:
  0.0 0.0 copy-start
  0.0 10.1 %forward.1 = bf16[160,16,16]{2,1,0:T(8,128)(2,1)} custom-call(s32[640]{0:T(1024)} %ids.3, bf16[160,2,8,1281]{3,2,1,0:T(8,128)(2,1)} %spectral.1, bf16[160,8,1281]{2,1,0:T(8,128)(2,1)} %legendre.3), custom_call_target="tpu_custom_call" | custom-call | tf_op jit(solution)/shard_map/forward/pallas_call | solution.py:354
  10.2 1.6 %copy.6 = bf16[160,16,16]{0,2,1:T(8,128)(2,1)S(1)} copy(bf16[160,16,16]{2,1,0:T(8,128)(2,1)} %forward.1) | data formatting | bytes 163840 | tf_op jit(solution)/shard_map/forward/pallas_call | solution.py:354
  11.8 0.0 copy-done
  11.8 27.1 %middle.1 = bf16[4,64,160]{2,1,0:T(8,128)(2,1)S(1)} custom-call(bf16[4,64,160]{2,1,0:T(8,128)(2,1)S(1)} %bitcast.8, s32[640]{0:T(1024)S(1)} %copy-done), custom_call_target="tpu_custom_call" | custom-call | tf_op jit(solution)/shard_map/middle/pallas_call | solution.py:239
  38.9 1.4 %copy.9.back = bf16[160,16,16]{2,1,0:T(8,128)(2,1)} copy(bf16[160,16,16]{0,1,2:T(8,128)(2,1)S(1)} %bitcast.11) | data formatting | bytes 163840 | tf_op jit(solution)/shard_map/reshape | solution.py:369
  40.3 7.4 %inverse.1 = bf16[160,2,8,1281]{3,2,1,0:T(8,128)(2,1)} custom-call(s32[640]{0:T(1024)} %ids.3, bf16[160,16,16]{2,1,0:T(8,128)(2,1)} %copy.9.back, bf16[160,8,1281]{2,1,0:T(8,128)(2,1)} %legendre.3), custom_call_target="tpu_custom_call" | custom-call | tf_op jit(solution)/shard_map/inverse/pallas_call | solution.py:370
  (2 shorter events, 0.0 us)
Async XLA Ops:
  0.0 11.8 %copy-start = (s32[640]{0:T(1024)S(1)}, s32[640]{0:T(1024)}, u32[]{:S(2)}) copy-start(s32[640]{0:T(1024)} %ids.3) | copy-start | bytes 7684
where the time goes:
time: 48.1 us; the launch traced here: 47.9 us
  Pallas kernels  44.7 us (93%)
  local copies, waits for them, and re-layouts  2.99 us (6%)
    pallas_call x1, Pallas kernels, middle(): pl.pallas_call(functools.partial(middle_kernel, waves, tiles, cols, lat_c...  27.1 us
    pallas_call x1, Pallas kernels, local(): pl.pallas_call(functools.partial(forward_kernel, take), out_shape=jax.Sha...  10.1 us
    pallas_call x1, Pallas kernels, local(): pl.pallas_call(functools.partial(inverse_kernel, take), out_shape=jax.Sha...  7.44 us
    pallas_call x1, local copies, waits for them, and re-layouts, local(): pl.pallas_call(functools.partial(forward_kernel, take), out_shape=jax.Sha...  1.58 us
    reshape x1, local copies, waits for them, and re-layouts, local(): back = back.reshape(slots, 2 * cols, 2 * lat_count)  1.39 us

commit v1 on v0

--- a/solution.py
+++ b/solution.py
@@ -380,8 +380,176 @@
     )(pair_ids, back, legendre)
 
 
+ROWS = 16
+UNIT = 8
+
+
+def iota(shape, axis):
+    return lax.broadcasted_iota(jnp.int32, shape, axis)
+
+
+def split_rows(ids, block, base):
+    count, lats, width = block.shape
+    lower = iota((2 * lats, width), 0) < lats
+    lane = iota((2 * lats, width), 1)
+    pattern = jnp.where(lower, lane, -lane).astype(jnp.int16)
+    side = iota((2 * lats, 1), 0) < lats
+    parts = []
+    for b in range(count):
+        bound = MW - ids[base + b]
+        limit = jnp.where(side, bound, 1 - bound).astype(jnp.int16)
+        both = jnp.concatenate([block[b], block[b]])
+        parts.append(jnp.where(pattern < limit, both, jnp.zeros((), BF16)))
+    return jnp.concatenate(parts)
+
+
+def lane_parts(shape, axis, waves, cols):
+    lane = iota(shape, axis)
+    lat = lane // cols % 2 + lane // (8 * cols) * 2
+    field = lane % cols + lane // (2 * cols) % 2 * cols
+    half = lane // (4 * cols) % 2
+    return half * (2 * waves) + lat, field
+
+
+def wide_forward_kernel(
+    take, waves, ids, spectral, legendre, out, spec_v, leg_v, mid, spec_sem, leg_sem
+):
+    slots, lats, width = legendre.shape
+    cols = spectral.shape[2]
+    fields = 2 * cols
+    base = lax.axis_index("wave") * slots
+    copies = []
+    for g in range(slots // take):
+        at = pl.ds(g * take, take)
+        copies.append([
+            pltpu.make_async_copy(legendre.at[at], leg_v.at[at], leg_sem.at[g]),
+            pltpu.make_async_copy(spectral.at[at], spec_v.at[at], spec_sem.at[g]),
+        ])
+        for copy in copies[-1]:
+            copy.start()
+    n = UNIT * ROWS
+    lanes = out.shape[1]
+    same = same_slot((n, n), ROWS, ROWS)
+    row_lane, field_lane = lane_parts((n, lanes), 1, waves, cols)
+    spread = jnp.where(iota((n, lanes), 0) % ROWS == field_lane, 1.0, 0.0).astype(BF16)
+    keep = iota((n, lanes), 0) % ROWS == row_lane
+    gather = jnp.where(iota((ROWS, 2 * n), 0) == iota((ROWS, 2 * n), 1) // ROWS, 1.0, 0.0)
+    gather = gather.astype(BF16)
+
+    def finish(g):
+        for at in range(g * take, (g + 1) * take, 2 * UNIT):
+            parts = []
+            for e in (at, at + UNIT):
+                part = dot(mid[e * ROWS : e * ROWS + n], spread)
+                parts.append(jnp.where(keep, part, 0.0).astype(BF16))
+            out[at : at + 2 * UNIT] = dot(gather, jnp.concatenate(parts)).astype(out.dtype)
+
+    for g, pair in enumerate(copies):
+        for copy in pair:
+            copy.wait()
+        if g:
+            finish(g - 1)
+        for at in range(g * take, (g + 1) * take, UNIT):
+            here = slice(at, at + UNIT)
+            left = split_rows(ids, leg_v[here], base + at)
+            right = spec_v[here].astype(F32).reshape(UNIT * fields, width).astype(BF16)
+            full = jnp.where(same, dot_nt(left, right), 0.0).astype(BF16)
+            mid[at * ROWS : at * ROWS + n] = full
+    finish(len(copies) - 1)
+
+
+def wide_inverse_kernel(
+    take, waves, ids, back, legendre, out, leg_v, out_v, mid, leg_sem, out_sem
+):
+    slots, lats, width = legendre.shape
+    cols = out.shape[2]
+    base = lax.axis_index("wave") * slots
+    copies = []
+    for g in range(slots // take):
+        at = pl.ds(g * take, take)
+        copies.append(pltpu.make_async_copy(legendre.at[at], leg_v.at[at], leg_sem.at[g]))
+        copies[-1].start()
+    n = UNIT * ROWS
+    lanes = back.shape[1]
+    same = same_slot((n, n), ROWS, ROWS)
+    row_lane, _ = lane_parts((lanes, n), 0, waves, cols)
+    spread = jnp.where(iota((lanes, n), 1) % ROWS == row_lane, 1.0, 0.0).astype(BF16)
+    _, field_lane = lane_parts((ROWS, lanes), 1, waves, cols)
+    keep = iota((ROWS, lanes), 0) == field_lane
+
+    def prepare(g):
+        for at in range(g * take, (g + 1) * take, UNIT):
+            rows = []
+            for b in range(at, at + UNIT):
+                row = jnp.broadcast_to(back[b : b + 1, :], (ROWS, lanes))
+                rows.append(jnp.where(keep, row, 0.0).astype(BF16))
+            wide = jnp.where(same, dot(jnp.concatenate(rows), spread), 0.0)
+            mid[at * ROWS : at * ROWS + n] = wide.astype(BF16)
+
+    prepare(0)
+    results = []
+    for g, copy in enumerate(copies):
+        copy.wait()
+        if g + 1 < len(copies):
+            prepare(g + 1)
+        for at in range(g * take, (g + 1) * take, UNIT):
+            here = slice(at, at + UNIT)
+            right = split_rows(ids, leg_v[here], base + at)
+            res = dot(mid[at * ROWS : at * ROWS + n], right)
+            out_v[here] = res.reshape((UNIT,) + out.shape[1:]).astype(BF16)
+        at = pl.ds(g * take, take)
+        results.append(pltpu.make_async_copy(out_v.at[at], out.at[at], out_sem.at[g]))
+        results[-1].start()
+    for copy in results:
+        copy.wait()
+
+
+def wide_local(spectral, legendre, pair_ids):
+    slots, _, cols, row_total = spectral.shape
+    lat_count = legendre.shape[1]
+    waves, tiles = lax.axis_size("wave"), lax.axis_size("tile")
+    take = 4 * UNIT
+    lanes = 4 * lat_count * cols
+    smem = pl.BlockSpec(memory_space=pltpu.SMEM)
+    vmem = pl.BlockSpec(memory_space=pltpu.VMEM)
+    hbm = pl.BlockSpec(memory_space=pl.ANY)
+    dma = pltpu.SemaphoreType.DMA((slots // take,))
+    params = pltpu.CompilerParams(vmem_limit_bytes=60 * 2**20)
+    scratch = [
+        pltpu.VMEM(spectral.shape, BF16), pltpu.VMEM((slots * ROWS, UNIT * ROWS), BF16), dma, dma
+    ]
+    leg_v = pltpu.VMEM(legendre.shape, BF16)
+    coef = pl.pallas_call(
+        functools.partial(wide_forward_kernel, take, waves),
+        out_shape=jax.ShapeDtypeStruct((slots, lanes), BF16),
+        in_specs=[smem, hbm, hbm],
+        out_specs=vmem,
+        scratch_shapes=[scratch[0], leg_v] + scratch[1:],
+        compiler_params=params,
+        name="forward",
+    )(pair_ids, spectral, legendre)
+    coef = coef.T.reshape(waves, 8 * cols, slots)
+    back = middle(coef, pair_ids, waves, tiles, cols, lat_count)
+    back = back.reshape(lanes, slots).T.astype(F32)
+    return pl.pallas_call(
+        functools.partial(wide_inverse_kernel, take, waves),
+        out_shape=jax.ShapeDtypeStruct(spectral.shape, BF16),
+        in_specs=[smem, vmem, hbm],
+        out_specs=hbm,
+        scratch_shapes=[leg_v] + scratch,
+        compiler_params=params,
+        name="inverse",
+    )(pair_ids, back, legendre)
+
+
+def pick(spectral, legendre, pair_ids):
+    slots, _, cols, _ = spectral.shape
+    fits = 2 * cols == ROWS and 2 * legendre.shape[1] == ROWS and slots % (4 * UNIT) == 0
+    return (wide_local if fits else local)(spectral, legendre, pair_ids)
+
+
 def solution(mesh):
     placed = (P("wave", None, "tile", None), P("wave", None, None), P())
     return jax.shard_map(
-        local, mesh=mesh, in_specs=placed, out_specs=P("wave", None, "tile", None), check_vma=False
+        pick, mesh=mesh, in_specs=placed, out_specs=P("wave", None, "tile", None), check_vma=False
     )

time: 48.1 us -> 43.1 us (0.90)
  Pallas kernels: 44.7 us -> 41.1 us
  local copies, waits for them, and re-layouts: 2.99 us -> 1.76 us
    pallas_call x2, Pallas kernels: 17.6 us -> 14 us  [the longest x1 7.89 us: wide_local(): pl.pallas_call(functools.partial(wide_forward_kernel, take, waves), out_s...]
    pallas_call x1 -> x0, local copies, waits for them, and re-layouts: 1.58 us -> none  [local(): pl.pallas_call(functools.partial(forward_kernel, take), out_shape=jax.Sha...]
    reshape x2 -> x0, local copies, waits for them, and re-layouts: 1.4 us -> none  [the longest x1 1.39 us: local(): back = back.reshape(slots, 2 * cols, 2 * lat_count)]
    transpose x1, local copies, waits for them, and re-layouts: 0.01 us -> 0.99 us  [wide_local(): coef = coef.T.reshape(waves, 8 * cols, slots)]
    convert_element_type x0 -> x1, local copies, waits for them, and re-layouts: none -> 0.77 us  [wide_local(): back = back.reshape(lanes, slots).T.astype(F32)]
where the time goes in v1:
time: 43.1 us; the launch traced here: 42.9 us
  Pallas kernels  41.1 us (95%)
  local copies, waits for them, and re-layouts  1.76 us (4%)
    pallas_call x1, Pallas kernels, middle(): pl.pallas_call(functools.partial(middle_kernel, waves, tiles, cols, lat_c...  27.1 us
    pallas_call x1, Pallas kernels, wide_local(): pl.pallas_call(functools.partial(wide_forward_kernel, take, waves), out_s...  7.89 us
    pallas_call x1, Pallas kernels, wide_local(): pl.pallas_call(functools.partial(wide_inverse_kernel, take, waves), out_s...  6.13 us
    transpose x1, local copies, waits for them, and re-layouts, wide_local(): coef = coef.T.reshape(waves, 8 * cols, slots)  0.99 us

profile of v1, /device:TPU:0, one launch (start us, length us, event | category | flops | bytes accessed | tf_op | source)
XLA Modules:
  0.0 42.9 jit_solution(18323867951861422345)
XLA Ops:
  0.0 0.0 copy-start
  0.0 7.9 %forward.1 = bf16[160,256]{1,0:T(8,128)(2,1)} custom-call(s32[640]{0:T(1024)} %ids.3, bf16[160,2,8,1281]{3,2,1,0:T(8,128)(2,1)} %spectral.1, bf16[160,8,1281]{2,1,0:T(8,128)(2,1)} %legendre.3), custom_call_target="tpu_custom_call" | custom-call | tf_op jit(solution)/shard_map/forward/pallas_call | solution.py:522
  7.9 1.0 %copy.6 = bf16[256,160]{1,0:T(8,128)(2,1)S(1)} copy(bf16[256,160]{0,1:T(8,128)(2,1)} %bitcast.8) | data formatting | bytes 163840 | tf_op jit(solution)/shard_map/transpose | solution.py:531
  8.9 0.0 copy-done
  8.9 27.1 %middle.1 = bf16[4,64,160]{2,1,0:T(8,128)(2,1)S(1)} custom-call(bf16[4,64,160]{2,1,0:T(8,128)(2,1)S(1)} %bitcast.6, s32[640]{0:T(1024)S(1)} %copy-done), custom_call_target="tpu_custom_call" | custom-call | tf_op jit(solution)/shard_map/middle/pallas_call | solution.py:239
  36.0 0.8 %copy.7 = f32[256,160]{0,1:T(8,128)} copy(f32[256,160]{1,0:T(8,128)S(1)} %bitcast_convert_fusion) | data formatting | bytes 327680 | tf_op jit(solution)/shard_map/convert_element_type | solution.py:533
  36.8 6.1 %inverse.1 = bf16[160,2,8,1281]{3,2,1,0:T(8,128)(2,1)} custom-call(s32[640]{0:T(1024)} %ids.3, f32[160,256]{1,0:T(8,128)} %bitcast.7, bf16[160,8,1281]{2,1,0:T(8,128)(2,1)} %legendre.3), custom_call_target="tpu_custom_call" | custom-call | tf_op jit(solution)/shard_map/inverse/pallas_call | solution.py:534
  (1 shorter events, 0.0 us)
Async XLA Ops:
  0.0 8.9 %copy-start = (s32[640]{0:T(1024)S(1)}, s32[640]{0:T(1024)}, u32[]{:S(2)}) copy-start(s32[640]{0:T(1024)} %ids.3) | copy-start | bytes 7684

commit v2 on v1

--- a/solution.py
+++ b/solution.py
@@ -412,12 +412,15 @@
 
 
 def wide_forward_kernel(
-    take, waves, ids, spectral, legendre, out, spec_v, leg_v, mid, spec_sem, leg_sem
+    take, waves, ids_in, spectral, legendre, out,
+    spec_v, leg_v, mid, spec_sem, leg_sem, ids, ids_sem
 ):
     slots, lats, width = legendre.shape
     cols = spectral.shape[2]
     fields = 2 * cols
     base = lax.axis_index("wave") * slots
+    ids_copy = pltpu.make_async_copy(ids_in, ids, ids_sem)
+    ids_copy.start()
     copies = []
     for g in range(slots // take):
         at = pl.ds(g * take, take)
@@ -444,6 +447,7 @@
                 parts.append(jnp.where(keep, part, 0.0).astype(BF16))
             out[at : at + 2 * UNIT] = dot(gather, jnp.concatenate(parts)).astype(out.dtype)
 
+    ids_copy.wait()
     for g, pair in enumerate(copies):
         for copy in pair:
             copy.wait()
@@ -459,11 +463,14 @@
 
 
 def wide_inverse_kernel(
-    take, waves, ids, back, legendre, out, leg_v, out_v, mid, leg_sem, out_sem
+    take, waves, ids_in, back, legendre, out,
+    leg_v, out_v, mid, leg_sem, out_sem, ids, ids_sem
 ):
     slots, lats, width = legendre.shape
     cols = out.shape[2]
     base = lax.axis_index("wave") * slots
+    ids_copy = pltpu.make_async_copy(ids_in, ids, ids_sem)
+    ids_copy.start()
     copies = []
     for g in range(slots // take):
         at = pl.ds(g * take, take)
@@ -487,6 +494,7 @@
             mid[at * ROWS : at * ROWS + n] = wide.astype(BF16)
 
     prepare(0)
+    ids_copy.wait()
     results = []
     for g, copy in enumerate(copies):
         copy.wait()
@@ -504,37 +512,316 @@
         copy.wait()
 
 
+def sine_turns(y):
+    z = y * y
+    terms = [(-1) ** i * (2.0 * math.pi) ** (2 * i + 1) / math.factorial(2 * i + 1) for i in range(6)]
+    acc = jnp.full_like(z, terms[-1])
+    for term in terms[-2::-1]:
+        acc = acc * z + term
+    return acc * y
+
+
+def turn_trig(whole, length):
+    inverse = 1.0 / length
+    rest = whole - jnp.round(whole * inverse) * length
+    x = rest * inverse
+    size = jnp.abs(x)
+    sine = sine_turns(0.25 - jnp.abs(size - 0.25))
+    return sine_turns(0.25 - size), jnp.where(x < 0.0, -sine, sine)
+
+
+def wide_middle_kernel(waves, tiles, cols, lat_count, rows, full_rows, *refs):
+    (coef, ids_in, out, wsend, fx, gsend, grecv, psend, precv, bsend, brecv, tab, hot, mix,
+     weights, low_c, low_s, base_c, base_s, ids, ids_sem, s1, r1, s2, r2, s3, r3, s4, r4) = refs
+    wave, tile = lax.axis_index("wave"), lax.axis_index("tile")
+    slots = coef.shape[0]
+    span = coef.shape[1] // waves
+    packed = LANES // span
+    part = slots // packed
+    quarter = HALF // 4
+    pairs = HALF
+    chunk = full_rows // 2 // tiles
+    half_rows = full_rows // 2
+    block = ROWS
+    blocks = rows // block
+
+    def exchange(axis, here, count, src, dst, send, recv):
+        copies = []
+        for off in range(1, count):
+            peer = lax.rem(here + off, count)
+            copy = pltpu.make_async_remote_copy(
+                src_ref=src.at[peer], dst_ref=dst.at[here], send_sem=send.at[off],
+                recv_sem=recv.at[off], device_id={axis: peer}, device_id_type=MESH,
+            )
+            copy.start()
+            copies.append(copy)
+        dst[here] = src[here]
+        return copies
+
+    def finish(axis, here, count, src, dst, send, recv):
+        for off in range(1, count):
+            origin = lax.rem(here + count - off, count)
+            pltpu.make_async_remote_copy(
+                src_ref=src.at[origin], dst_ref=dst.at[origin], send_sem=send.at[off],
+                recv_sem=recv.at[off], device_id={axis: origin}, device_id_type=MESH,
+            ).wait_recv()
+
+    ids_copy = pltpu.make_async_copy(ids_in, ids, ids_sem)
+    ids_copy.start()
+    barrier = pltpu.get_barrier_semaphore()
+    for axis, here, count in (("wave", wave, waves), ("tile", tile, tiles)):
+        for off in range(1, count):
+            pl.semaphore_signal(
+                barrier, inc=1, device_id={axis: lax.rem(here + off, count)}, device_id_type=MESH
+            )
+
+    lane = iota((1, LANES), 1)
+    for w in range(waves):
+        at = w * span // LANES * LANES
+        place = w * span % LANES // span
+        piece = None
+        for j in range(packed):
+            x = coef[j * part : (j + 1) * part, at : at + LANES].astype(F32)
+            if j != place:
+                x = pltpu.roll(x, (j - place) * span % LANES, 1)
+            piece = x if piece is None else jnp.where(lane // span == j, x, piece)
+        wsend[w] = piece.astype(BF16)
+
+    polar = wave * HALF // (lat_count // 2)
+    n0, n1 = 20 + 4 * polar, 20 + 4 * (HALF_LATS - 1 - polar)
+    count0, count1 = n0 // 8 + 1, n1 // 8 + 1
+    first = (count0 + block - 1) // block
+    start1 = first * block
+
+    j = iota((1, 2 * pairs), 1)
+    upper = j >= pairs
+    order = j - jnp.where(upper, pairs, 0)
+    q = 4 * (order % quarter) + order // quarter
+    number = jnp.where(upper, MW - 1 - q, q)
+    m = number.astype(F32)
+    row = iota((2 * block, 1), 0)
+    low_n = jnp.where(row >= block, n1, n0).astype(F32)
+    low_c[...], low_s[...] = turn_trig((row % block).astype(F32) * m, low_n)
+
+    pl.semaphore_wait(barrier, waves + tiles - 2)
+    sends = exchange("wave", wave, waves, wsend, fx, s1, r1)
+
+    row = iota((base_c.shape[0], 1), 0)
+    base_k = block * jnp.where(row >= first, row - first, row)
+    base_n = jnp.where(row >= first, n1, n0).astype(F32)
+    base_c[...], base_s[...] = turn_trig(base_k.astype(F32) * m, base_n)
+
+    def fill(b, carry):
+        later = (b - first + 2 * blocks) // (2 * blocks)
+        low = pl.ds(pl.multiple_of(later * block, block), block)
+        at = pl.ds(pl.multiple_of(b * block, block), block)
+        ac, as_ = base_c[pl.ds(b, 1), :], base_s[pl.ds(b, 1), :]
+        bc, bs = low_c[low, :], low_s[low, :]
+        tab[at, : 2 * pairs] = (ac * bc - as_ * bs).astype(BF16)
+        tab[at, 2 * pairs :] = (as_ * bc + ac * bs).astype(BF16)
+        return carry
+
+    lax.fori_loop(0, blocks, fill, 0, unroll=2)
+
+    ids_copy.wait()
+    pair = ids[...].reshape(1, ids.shape[0])
+    place = iota((pairs, 1), 0)
+    hot[...] = jnp.where(pair == 4 * (place % quarter) + place // quarter, 1.0, 0.0).astype(BF16)
+
+    shape = (4 * cols, 2 * LANES)
+    src, dst = iota(shape, 0), iota(shape, 1)
+    same_col = src % (2 * cols) == dst % (2 * cols)
+    start = src // (2 * cols) + dst // LANES * (1 + 2 * (dst // (2 * cols) % 2))
+    start = jnp.where(same_col, start, 1)
+    step = jnp.where(same_col, dst % LANES // (4 * cols), 0)
+    for r in range(4):
+        v = (start + r * step) % 4
+        rule = jnp.where(v == 0, 2.0, jnp.where(v == 2, -2.0, 0.0)).astype(BF16)
+        blank = jnp.zeros_like(rule)
+        mix[0, r] = jnp.concatenate([rule, blank] * packed)
+        mix[1, 3 - r] = jnp.concatenate([blank, rule] * packed)
+
+    lat_lane = lane // cols % 2
+    n_lane = jnp.where(lat_lane == 1, n1, n0)
+    four_i = 4 * iota((quarter, 1), 0)
+
+    point = iota((half_rows, 1), 0) + half_rows * lat_lane
+    k_point = jnp.where(point >= start1, point - start1, point)
+    n_point = jnp.where(point >= start1, n1, n0)
+    twice = (k_point == 0) | (8 * k_point == n_point)
+    used = 8 * k_point <= n_point
+    used = used & jnp.logical_not(twice & (lane // (2 * cols) % 2 == 1))
+    used = jnp.where(used & (point < rows), 1.0, 0.0).astype(BF16)
+
+    src, dst = iota((LANES, LANES), 0), iota((LANES, LANES), 1)
+    kind = dst // (2 * cols)
+    src_turn = src // (4 * cols)
+    base_turn = jnp.where(kind % 4 == 3, jnp.where(kind < 4, 1, 0), jnp.where(kind == 6, 1, 0))
+    even_sign = jnp.where(src_turn % 2 == 1, -1.0, 1.0)
+    diff = jnp.where(src_turn == base_turn, 1.0, jnp.where(src_turn == base_turn + 2, -1.0, 0.0))
+    gain = jnp.where(kind % 4 == 0, 1.0, jnp.where(kind % 4 == 1, even_sign, diff))
+    gain = jnp.where((kind >= 4) & (src // (2 * cols) % 2 == 1), -gain, gain)
+    gain = jnp.where(src % cols == dst % cols, gain, 0.0)
+    second_half = src // cols % 2 == 1
+    folding = [jnp.where(second_half, 0.0, gain), jnp.where(second_half, gain, 0.0)]
+    folding = jnp.concatenate(folding, axis=1).astype(BF16)
+
+    levels = iota((LANES, LANES), 0), iota((LANES, LANES), 1)
+    same_point = levels[0] // cols == levels[1] // cols
+    above = jnp.where(same_point, 1.0, 0.0).astype(BF16)
+    within = jnp.where(same_point & (levels[0] % cols >= levels[1] % cols), 1.0, 0.0).astype(BF16)
+
+    finish("wave", wave, waves, wsend, fx, s1, r1)
+    pieces = []
+    for w in range(waves):
+        x = fx[w]
+        for p in range(packed):
+            pieces.append(jnp.where(lane // span == p, x, jnp.zeros((), BF16)))
+    sorted_in = dot(hot[...], jnp.concatenate(pieces)).astype(BF16)
+    for h in range(2):
+        for r in range(4):
+            x = dot(sorted_in[r * quarter : (r + 1) * quarter], mix[h, r])
+            at = h * pairs + r * quarter
+            col_m = four_i + r if h == 0 else MW - 1 - r - four_i
+            inside = 2 * col_m < n_lane
+            for x in (x[:, :LANES], x[:, LANES:]):
+                if h == 0 and r == 0:
+                    x = jnp.where(col_m == 0, 0.5 * x, x)
+                weights[at : at + quarter] = jnp.where(inside, x, 0.0).astype(BF16)
+                at += 2 * pairs
+    high = dot(tab[half_rows:], weights[...])
+    high = jnp.concatenate([high, jnp.zeros((full_rows - rows, LANES), F32)])
+    low = dot(tab[:half_rows], weights[...])
+    row = iota((half_rows, 1), 0)
+    low = jnp.where(row >= start1, pltpu.roll(low, LANES - cols, 1), low)
+    high = jnp.where(row + half_rows >= start1, high, pltpu.roll(high, cols, 1))
+    both = jnp.where(lat_lane == 0, low, high).astype(BF16)
+    for t in range(tiles):
+        gsend[t] = both[t * chunk : (t + 1) * chunk]
+    sends += exchange("tile", tile, tiles, gsend, grecv, s2, r2)
+    finish("tile", tile, tiles, gsend, grecv, s2, r2)
+
+    per_f = tiles // 4
+    layers = cols * per_f
+    for t in range(per_f):
+        u, w_ = grecv[t].astype(F32), grecv[per_f + t].astype(F32)
+        t16 = grecv[2 * per_f + t]
+        geo = dot(t16, within)
+        for other in range(t + 1, per_f):
+            geo = geo + dot(grecv[2 * per_f + other], above)
+        temp, wet = t16.astype(F32), grecv[3 * per_f + t].astype(F32)
+        energy = 0.5 * (u * u + w_ * w_) + geo / math.sqrt(layers)
+        for f, x in enumerate((energy, u * temp, w_ * temp, u * wet)):
+            psend[f * per_f + t] = x.astype(BF16)
+    sends += exchange("tile", tile, tiles, psend, precv, s3, r3)
+
+    row = iota((2 * cols, 1), 0)
+    n_row = jnp.where(row >= cols, n1, n0)
+    cycle = jnp.where(row >= cols, HALF_LATS - 1 - polar, polar)
+    weight = 40.0 * jnp.sin(math.pi * (cycle.astype(F32) + 0.5) / (2.0 * HALF_LATS))
+    weight = weight / jnp.sqrt(lat_count * n_row.astype(F32))
+    weight = jnp.where(2 * number < n_row, weight, 0.0)
+    residue = number % 4
+    point = iota((LANES, full_rows), 1)
+    lat_row = iota((LANES, full_rows), 0) // cols % 2
+    own = (lat_row == 1) == (point >= start1)
+
+    finish("tile", tile, tiles, psend, precv, s3, r3)
+    back = jnp.concatenate([precv[t] for t in range(tiles)]) * used
+    back = dot(back, folding)
+    back = jnp.concatenate([back[:, :LANES], back[:, LANES:]]).T
+    back = jnp.where(own, back, 0.0).astype(BF16)[:, :rows]
+    cos_out = dot(back[: LANES // 2], tab[:, : 2 * pairs])
+    sin_out = dot(back[LANES // 2 :], tab[:, 2 * pairs :])
+    step = 2 * cols
+    c0, c1, c2, c3 = [cos_out[i * step : (i + 1) * step] for i in range(4)]
+    d0, d1, d2, d3 = [sin_out[i * step : (i + 1) * step] for i in range(4)]
+    is0, is1, is2 = residue == 0, residue == 1, residue == 2
+    real = jnp.where(is0, c0, jnp.where(is2, c1, c2 + jnp.where(is1, -d2, d2))) * weight
+    other = jnp.where(is0, -d0, jnp.where(is2, -d1, jnp.where(is1, -c3, c3) - d3)) * weight
+    rows_out = jnp.concatenate(
+        [x[:, h * pairs : (h + 1) * pairs] for h in range(2) for x in (real, other)]
+    ).astype(BF16)
+    res = dot(rows_out, hot[...]).astype(BF16)
+    for w in range(waves):
+        bsend[w] = res[:, w * slots : (w + 1) * slots]
+    sends += exchange("wave", wave, waves, bsend, brecv, s4, r4)
+    finish("wave", wave, waves, bsend, brecv, s4, r4)
+    result = jnp.concatenate([brecv[w].astype(F32) for w in range(waves)])
+    out[...] = result.T
+    for copy in sends:
+        copy.wait_send()
+
+
+def wide_middle(coef, ids, waves, tiles, cols, lat_count):
+    slots, lanes = coef.shape
+    span = lanes // waves
+    packed = LANES // span
+    rows = (NPTS // 8 + 2 + 2 * (ROWS - 1)) // ROWS * ROWS
+    unit = 2 * tiles * ROWS
+    full_rows = -(-rows // unit) * unit
+    base_rows = -(-(rows // ROWS) // 8) * 8
+    dma = pltpu.SemaphoreType.DMA
+    vmem = pl.BlockSpec(memory_space=pltpu.VMEM)
+    first = (waves, slots // packed, LANES)
+    chunk = (tiles, full_rows // 2 // tiles, LANES)
+    last = (waves, span, slots)
+    return pl.pallas_call(
+        functools.partial(wide_middle_kernel, waves, tiles, cols, lat_count, rows, full_rows),
+        out_shape=jax.ShapeDtypeStruct((slots, lanes), F32),
+        in_specs=[vmem, pl.BlockSpec(memory_space=pltpu.HBM)],
+        out_specs=vmem,
+        scratch_shapes=[
+            pltpu.VMEM(first, BF16), pltpu.VMEM(first, BF16),
+            pltpu.VMEM(chunk, BF16), pltpu.VMEM(chunk, BF16),
+            pltpu.VMEM(chunk, BF16), pltpu.VMEM(chunk, BF16),
+            pltpu.VMEM(last, BF16), pltpu.VMEM(last, BF16),
+            pltpu.VMEM((rows, 4 * HALF), BF16),
+            pltpu.VMEM((HALF, waves * slots), BF16),
+            pltpu.VMEM((2, 4, LANES, 2 * LANES), BF16),
+            pltpu.VMEM((4 * HALF, LANES), BF16),
+            pltpu.VMEM((2 * ROWS, 2 * HALF), F32), pltpu.VMEM((2 * ROWS, 2 * HALF), F32),
+            pltpu.VMEM((base_rows, 2 * HALF), F32), pltpu.VMEM((base_rows, 2 * HALF), F32),
+            pltpu.VMEM(ids.shape, jnp.int32), dma,
+            dma((waves,)), dma((waves,)), dma((tiles,)), dma((tiles,)),
+            dma((tiles,)), dma((tiles,)), dma((waves,)), dma((waves,)),
+        ],
+        compiler_params=pltpu.CompilerParams(
+            collective_id=0, has_side_effects=True, vmem_limit_bytes=40 * 2**20
+        ),
+        name="middle",
+    )(coef, ids)
+
+
 def wide_local(spectral, legendre, pair_ids):
     slots, _, cols, row_total = spectral.shape
     lat_count = legendre.shape[1]
     waves, tiles = lax.axis_size("wave"), lax.axis_size("tile")
     take = 4 * UNIT
     lanes = 4 * lat_count * cols
-    smem = pl.BlockSpec(memory_space=pltpu.SMEM)
     vmem = pl.BlockSpec(memory_space=pltpu.VMEM)
-    hbm = pl.BlockSpec(memory_space=pl.ANY)
+    hbm = pl.BlockSpec(memory_space=pltpu.HBM)
     dma = pltpu.SemaphoreType.DMA((slots // take,))
-    params = pltpu.CompilerParams(vmem_limit_bytes=60 * 2**20)
+    params = pltpu.CompilerParams(vmem_limit_bytes=52 * 2**20)
     scratch = [
-        pltpu.VMEM(spectral.shape, BF16), pltpu.VMEM((slots * ROWS, UNIT * ROWS), BF16), dma, dma
+        pltpu.VMEM(spectral.shape, BF16), pltpu.VMEM((slots * ROWS, UNIT * ROWS), BF16), dma, dma,
+        pltpu.SMEM(pair_ids.shape, jnp.int32), pltpu.SemaphoreType.DMA,
     ]
     leg_v = pltpu.VMEM(legendre.shape, BF16)
     coef = pl.pallas_call(
         functools.partial(wide_forward_kernel, take, waves),
         out_shape=jax.ShapeDtypeStruct((slots, lanes), BF16),
-        in_specs=[smem, hbm, hbm],
+        in_specs=[hbm, hbm, hbm],
         out_specs=vmem,
         scratch_shapes=[scratch[0], leg_v] + scratch[1:],
         compiler_params=params,
         name="forward",
     )(pair_ids, spectral, legendre)
-    coef = coef.T.reshape(waves, 8 * cols, slots)
-    back = middle(coef, pair_ids, waves, tiles, cols, lat_count)
-    back = back.reshape(lanes, slots).T.astype(F32)
+    back = wide_middle(coef, pair_ids, waves, tiles, cols, lat_count)
     return pl.pallas_call(
         functools.partial(wide_inverse_kernel, take, waves),
         out_shape=jax.ShapeDtypeStruct(spectral.shape, BF16),
-        in_specs=[smem, vmem, hbm],
+        in_specs=[hbm, vmem, hbm],
         out_specs=hbm,
         scratch_shapes=[leg_v] + scratch,
         compiler_params=params,
@@ -545,6 +832,7 @@
 def pick(spectral, legendre, pair_ids):
     slots, _, cols, _ = spectral.shape
     fits = 2 * cols == ROWS and 2 * legendre.shape[1] == ROWS and slots % (4 * UNIT) == 0
+    fits = fits and lax.axis_size("wave") * 2 == legendre.shape[1]
     return (wide_local if fits else local)(spectral, legendre, pair_ids)
 
 

time: 43.1 us -> 36.6 us (0.85)
  Pallas kernels: 41.1 us -> 35.7 us
  local copies, waits for them, and re-layouts: 1.76 us -> 0.69 us
    pallas_call x1, Pallas kernels: 27.1 us -> 24 us  [wide_middle(): pl.pallas_call(functools.partial(wide_middle_kernel, waves, tiles, cols,...]
    pallas_call x1, Pallas kernels: 7.89 us -> 6.44 us  [wide_local(): pl.pallas_call(functools.partial(wide_forward_kernel, take, waves), out_s...]
    transpose x1 -> x0, local copies, waits for them, and re-layouts: 0.99 us -> none  [wide_local(): coef = coef.T.reshape(waves, 8 * cols, slots)]
    pallas_call x1, Pallas kernels: 6.13 us -> 5.24 us  [wide_local(): pl.pallas_call(functools.partial(wide_inverse_kernel, take, waves), out_s...]
    convert_element_type x1 -> x0, local copies, waits for them, and re-layouts: 0.77 us -> none  [wide_local(): back = back.reshape(lanes, slots).T.astype(F32)]
    unnamed x2, local copies, waits for them, and re-layouts: 0.01 us -> 0.69 us
where the time goes in v2:
time: 36.6 us; the launch traced here: 36.4 us
  Pallas kernels  35.7 us (98%)
  local copies, waits for them, and re-layouts  0.69 us (2%)
    pallas_call x1, Pallas kernels, wide_middle(): pl.pallas_call(functools.partial(wide_middle_kernel, waves, tiles, cols,...  24 us
    pallas_call x1, Pallas kernels, wide_local(): pl.pallas_call(functools.partial(wide_forward_kernel, take, waves), out_s...  6.44 us
    pallas_call x1, Pallas kernels, wide_local(): pl.pallas_call(functools.partial(wide_inverse_kernel, take, waves), out_s...  5.24 us

profile of v2, /device:TPU:0, one launch (start us, length us, event | category | flops | bytes accessed | tf_op | source)
XLA Modules:
  0.0 36.4 jit_solution(6011681768127348211)
XLA Ops:
  0.0 0.0 copy-start
  0.0 0.7 %copy-done = s32[640]{0:T(1024)S(1)} copy-done((s32[640]{0:T(1024)S(1)}, s32[640]{0:T(1024)}, u32[]{:S(2)}) %copy-start) | copy-done | bytes 2584
  0.7 6.4 %forward.1.refs_0_ = bf16[160,256]{1,0:T(8,128)(2,1)S(1)} custom-call(s32[640]{0:T(1024)S(1)} %copy-done, bf16[160,2,8,1281]{3,2,1,0:T(8,128)(2,1)} %spectral.1, bf16[160,8,1281]{2,1,0:T(8,128)(2,1)} %legendre.3), custom_call_target="tpu_custom_call" | custom-call | tf_op jit(solution)/shard_map/forward/pallas_call | solution.py:811
  7.1 24.0 %middle.1.back = f32[160,256]{1,0:T(8,128)S(1)} custom-call(bf16[160,256]{1,0:T(8,128)(2,1)S(1)} %forward.1.refs_0_, s32[640]{0:T(1024)S(1)} %copy-done), custom_call_target="tpu_custom_call" | custom-call | tf_op jit(solution)/shard_map/middle/pallas_call | solution.py:769
  31.2 5.2 %inverse.1 = bf16[160,2,8,1281]{3,2,1,0:T(8,128)(2,1)} custom-call(s32[640]{0:T(1024)S(1)} %copy-done, f32[160,256]{1,0:T(8,128)S(1)} %middle.1.back, bf16[160,8,1281]{2,1,0:T(8,128)(2,1)} %legendre.3), custom_call_target="tpu_custom_call" | custom-call | tf_op jit(solution)/shard_map/inverse/pallas_call | solution.py:821
Async XLA Ops:
  0.0 0.7 %copy-start = (s32[640]{0:T(1024)S(1)}, s32[640]{0:T(1024)}, u32[]{:S(2)}) copy-start(s32[640]{0:T(1024)} %ids_in.3) | copy-start | bytes 7684

commit v3 on v2

--- a/solution.py
+++ b/solution.py
@@ -742,13 +742,25 @@
     rows_out = jnp.concatenate(
         [x[:, h * pairs : (h + 1) * pairs] for h in range(2) for x in (real, other)]
     ).astype(BF16)
-    res = dot(rows_out, hot[...]).astype(BF16)
+    res = dot(rows_out, hot[...])
+    whole = slots // LANES * LANES
+    rest = slots - whole
+    share = span * rest // LANES
     for w in range(waves):
-        bsend[w] = res[:, w * slots : (w + 1) * slots]
+        at = w * slots
+        bsend[w, :span] = res[:, at : at + whole].astype(BF16)
+        tail = res[:, at + whole : at + slots]
+        tail = [tail[e : e + share] for e in range(0, span, share)]
+        bsend[w, span:] = jnp.concatenate(tail, axis=1).astype(BF16)
     sends += exchange("wave", wave, waves, bsend, brecv, s4, r4)
     finish("wave", wave, waves, bsend, brecv, s4, r4)
-    result = jnp.concatenate([brecv[w].astype(F32) for w in range(waves)])
-    out[...] = result.T
+    body = jnp.concatenate([brecv[w, :span].astype(F32) for w in range(waves)])
+    out[:whole] = body.T
+    tails = []
+    for w in range(waves):
+        tail = brecv[w, span:].astype(F32)
+        tails += [tail[:, e : e + rest] for e in range(0, LANES, rest)]
+    out[whole:] = jnp.concatenate(tails).T
     for copy in sends:
         copy.wait_send()
 
@@ -765,7 +777,7 @@
     vmem = pl.BlockSpec(memory_space=pltpu.VMEM)
     first = (waves, slots // packed, LANES)
     chunk = (tiles, full_rows // 2 // tiles, LANES)
-    last = (waves, span, slots)
+    last = (waves, span * slots // LANES, LANES)
     return pl.pallas_call(
         functools.partial(wide_middle_kernel, waves, tiles, cols, lat_count, rows, full_rows),
         out_shape=jax.ShapeDtypeStruct((slots, lanes), F32),
@@ -833,6 +845,8 @@
     slots, _, cols, _ = spectral.shape
     fits = 2 * cols == ROWS and 2 * legendre.shape[1] == ROWS and slots % (4 * UNIT) == 0
     fits = fits and lax.axis_size("wave") * 2 == legendre.shape[1]
+    fits = fits and slots // LANES == 1 and LANES % max(slots % LANES, 1) == 0
+    fits = fits and slots % LANES >= 32
     return (wide_local if fits else local)(spectral, legendre, pair_ids)
 
 

time: 36.6 us -> 36.2 us (0.989)
  Pallas kernels: 35.7 us -> 35.3 us
where the time goes in v3:
time: 36.2 us; the launch traced here: 36 us
  Pallas kernels  35.3 us (98%)
  local copies, waits for them, and re-layouts  0.69 us (2%)
    pallas_call x1, Pallas kernels, wide_middle(): pl.pallas_call(functools.partial(wide_middle_kernel, waves, tiles, cols,...  23.7 us
    pallas_call x1, Pallas kernels, wide_local(): pl.pallas_call(functools.partial(wide_forward_kernel, take, waves), out_s...  6.44 us
    pallas_call x1, Pallas kernels, wide_local(): pl.pallas_call(functools.partial(wide_inverse_kernel, take, waves), out_s...  5.22 us

profile of v3, /device:TPU:0, one launch (start us, length us, event | category | flops | bytes accessed | tf_op | source)
XLA Modules:
  0.0 36.0 jit_solution(7187518304727679071)
XLA Ops:
  0.0 0.0 copy-start
  0.0 0.7 %copy-done = s32[640]{0:T(1024)S(1)} copy-done((s32[640]{0:T(1024)S(1)}, s32[640]{0:T(1024)}, u32[]{:S(2)}) %copy-start) | copy-done | bytes 2584
  0.7 6.4 %forward.1.refs_0_ = bf16[160,256]{1,0:T(8,128)(2,1)S(1)} custom-call(s32[640]{0:T(1024)S(1)} %copy-done, bf16[160,2,8,1281]{3,2,1,0:T(8,128)(2,1)} %spectral.1, bf16[160,8,1281]{2,1,0:T(8,128)(2,1)} %legendre.3), custom_call_target="tpu_custom_call" | custom-call | tf_op jit(solution)/shard_map/forward/pallas_call | solution.py:823
  7.1 23.7 %middle.1.back = f32[160,256]{1,0:T(8,128)S(1)} custom-call(bf16[160,256]{1,0:T(8,128)(2,1)S(1)} %forward.1.refs_0_, s32[640]{0:T(1024)S(1)} %copy-done), custom_call_target="tpu_custom_call" | custom-call | tf_op jit(solution)/shard_map/middle/pallas_call | solution.py:781
  30.8 5.2 %inverse.1 = bf16[160,2,8,1281]{3,2,1,0:T(8,128)(2,1)} custom-call(s32[640]{0:T(1024)S(1)} %copy-done, f32[160,256]{1,0:T(8,128)S(1)} %middle.1.back, bf16[160,8,1281]{2,1,0:T(8,128)(2,1)} %legendre.3), custom_call_target="tpu_custom_call" | custom-call | tf_op jit(solution)/shard_map/inverse/pallas_call | solution.py:833
Async XLA Ops:
  0.0 0.7 %copy-start = (s32[640]{0:T(1024)S(1)}, s32[640]{0:T(1024)}, u32[]{:S(2)}) copy-start(s32[640]{0:T(1024)} %ids_in.3) | copy-start | bytes 7684
